TPU v7x, 256 devices: a whole 4x4x8 slice. The times are simulated.
256 devices in a mesh: grp: 8 (over x, core), dev: 32 (over y, z).
Axes of the slice: x: 4, y: 4, z: 8, core: 2. Of those that a mesh axis runs over, the one named last changes fastest.
Arguments:
- tensor_slab: bfloat16 [512, 512, 64, 64], P(None, 'dev', 'grp'), may hold values from -400 to 400
- mode_factor: bfloat16 [512, 64], replicated, may hold values from -40 to 40
Outputs:
- triangle: float32 [512, 512], P('dev', 'grp')
All inputs are finite; a program needn't handle non-finite values.
Results may differ from a plain program's by a relative error of at most 0.00033.
Values may be sent and summed in bfloat16 or wider, within the bound.
A program may use at most 64 MiB of HBM per device.

v0:
```python
import jax
import jax.numpy as jnp
from jax import lax
from jax.sharding import PartitionSpec as P


def own_block(full_tri):
    order = full_tri.shape[0]
    row_count = order // lax.axis_size("dev")
    col_count = order // lax.axis_size("grp")
    row_start = lax.axis_index("dev") * row_count
    col_start = lax.axis_index("grp") * col_count
    return lax.dynamic_slice(full_tri, (row_start, col_start), (row_count, col_count))


def per_device(tensor_slab, mode_factor):
    row_width = tensor_slab.shape[0]
    local_cols = tensor_slab.shape[1]
    slab_depth = tensor_slab.shape[2]
    species = tensor_slab.shape[3]
    flat_slab = tensor_slab.reshape(row_width, local_cols * slab_depth * species)
    projected = lax.dot_general(
        mode_factor, flat_slab, (((0,), (0,)), ((), ())), preferred_element_type=jnp.float32
    )
    projected = projected.astype(jnp.bfloat16).reshape(
        mode_factor.shape[1], local_cols, slab_depth * species
    )
    regrouped = lax.all_to_all(projected, "dev", split_axis=0, concat_axis=1, tiled=True)
    gram_local = lax.dot_general(
        regrouped, regrouped, (((0, 2), (0, 2)), ((), ())), preferred_element_type=jnp.float32
    )
    row_total = mode_factor.shape[1] * slab_depth * species * lax.axis_size("grp")
    gram_local = gram_local / row_total
    gram_total = lax.psum(gram_local, ("grp", "dev"))
    return own_block(jnp.linalg.cholesky(gram_total).T)


def solution(mesh):
    in_specs = (P(None, "dev", "grp", None), P())
    out_specs = P("dev", "grp")
    return jax.shard_map(
        per_device, mesh=mesh, in_specs=in_specs, out_specs=out_specs, check_vma=False
    )
```

profile of v0, /device:TPU:1, one launch (start us, length us, event | category | flops | bytes accessed | tf_op | source)
XLA Modules:
  0.0 404.9 jit_solution(6353518399661913828)
XLA Ops:
  6.5 0.0 copy-start
  6.5 0.0 all-reduce.3.cloned.1.call-start
  6.5 0.8 copy-done
  7.4 6.0 %convolution_convert_fusion = bf16[64,8192]{1,0:T(8,128)(2,1)S(1)} fusion(bf16[512,64]{0,1:T(8,128)(2,1)S(1)} %copy-done, bf16[512,8192]{0,1:T(8,128)(2,1)} %bitcast.37), kind=kOutput, calls=%fused_computation | convolution fusion | flops 537395200 | bytes 9502720 | tf_op jit(solution)/shard_map/dot_general | solution.py:22
  13.4 0.4 copy.14
  13.7 36.7 %all_to_all.18 = bf16[64,16,512]{2,1,0:T(8,128)(2,1)S(1)} all-to-all(bf16[64,16,512]{2,1,0:T(8,128)(2,1)S(1)} %bitcast.38), channel_id=1, replica_groups=mesh['grp'=8,'dev'=32] {'dev'}, dimensions={0} | all-to-all | bytes 2097152 | tf_op jit(solution)/shard_map/all_to_all | solution.py:28
  50.4 0.1 copy.3
  50.5 1.8 fusion
  52.3 0.0 all-reduce.3.cloned.1.call-update
  52.3 258.3 %all-reduce.3.cloned.1.call-done = f32[512,512]{0,1:T(8,128)} async-done(((f32[512,512]{0,1:T(8,128)}), f32[512,512]{0,1:T(8,128)}) %all-reduce.3.cloned.1.call-update) | async-done | bytes 1048592 | tf_op jit(solution)/shard_map/psum | solution.py:34
  310.6 1.6 copy.5
  312.2 1.4 fusion.1
  313.7 11.7 %cholesky.104 = f32[128,128]{1,0:T(8,128)S(1)} custom-call(f32[128,128]{1,0:T(8,128)S(1)} %cholesky.266), custom_call_target="Cholesky" | custom-call | tf_op jit(solution)/shard_map/jit(cholesky)/cholesky | solution.py:35
  325.4 9.8 %custom-call.27 = f32[1,128,128]{1,2,0:T(8,128)S(1)} custom-call(f32[1,128,128]{2,1,0:T(8,128)S(1)} %get-tuple-element.14), custom_call_target="InvertDiagBlocksLowerTriangular" | custom-call | tf_op jit(solution)/shard_map/jit(cholesky)/cholesky | solution.py:35
  335.2 0.4 fusion.4
  335.7 0.1 copy.6
  335.8 0.5 convolution_subtract_fusion
  336.3 0.1 cholesky.224
  336.4 11.7 %cholesky.217 = f32[128,128]{1,0:T(8,128)S(1)} custom-call(f32[128,128]{1,0:T(8,128)S(1)} %cholesky.270), custom_call_target="Cholesky" | custom-call | tf_op jit(solution)/shard_map/jit(cholesky)/cholesky | solution.py:35
  348.2 9.9 %custom-call.28 = f32[1,128,128]{1,2,0:T(8,128)S(1)} custom-call(f32[1,128,128]{2,1,0:T(8,128)S(1)} %get-tuple-element.11), custom_call_target="InvertDiagBlocksLowerTriangular" | custom-call | tf_op jit(solution)/shard_map/jit(cholesky)/cholesky | solution.py:35
  358.1 0.3 convolution_dynamic-update-slice_fusion
  358.4 0.4 convolution_subtract_fusion.1
  358.8 11.7 %cholesky.238 = f32[128,128]{1,0:T(8,128)S(1)} custom-call(f32[128,128]{1,0:T(8,128)S(1)} %cholesky.275), custom_call_target="Cholesky" | custom-call | tf_op jit(solution)/shard_map/jit(cholesky)/cholesky | solution.py:35
  370.5 0.7 compare_reduce_fusion.1
  371.3 9.8 %custom-call.29 = f32[1,128,128]{1,2,0:T(8,128)S(1)} custom-call(f32[1,128,128]{2,1,0:T(8,128)S(1)} %get-tuple-element.8), custom_call_target="InvertDiagBlocksLowerTriangular" | custom-call | tf_op jit(solution)/shard_map/jit(cholesky)/cholesky | solution.py:35
  381.1 0.2 convolution_dynamic-update-slice_fusion.1
  381.3 0.4 convolution_subtract_fusion.2
  381.7 11.7 %cholesky.255 = f32[128,128]{1,0:T(8,128)S(1)} custom-call(f32[128,128]{1,0:T(8,128)S(1)} %convolution_subtract_fusion.2), custom_call_target="Cholesky" | custom-call | tf_op jit(solution)/shard_map/jit(cholesky)/cholesky | solution.py:35
  393.4 0.6 compare_reduce_fusion
  394.1 0.7 compare_reduce_fusion.2
  397.3 0.1 fusion.14
  397.4 0.7 copy.9
  (8 shorter events, 0.2 us)
Async XLA Ops:
  6.5 0.8 copy-start
  6.5 304.1 %all-reduce.3.cloned.1.call-start = ((), (), s32[]{:S(2)}) async-start(), calls=%async_computation.1 | async-start | bytes 2097152 | tf_op jit(solution)/shard_map/psum | solution.py:34
Sparse Core Ops, SparseCore 0:
  52.4 258.1 all-reduce.2
where the time goes:
time: 406 us; the launch traced here: 405 us
  waiting for transfers between devices  258 us (64%)
  other arithmetic  80.1 us (20%)
  blocking collectives  36.7 us (9%)
  between operations  16.1 us (4%)
  matrix products  9.91 us (2%)
    psum x1, waiting for transfers between devices, per_device(): gram_total = lax.psum(gram_local, ('grp', 'dev'))  258 us
    another operation x14, other arithmetic, per_device(): return own_block(jnp.linalg.cholesky(gram_total).T)  78.6 us
    all_to_all x1, blocking collectives, per_device(): lax.all_to_all(projected, 'dev', split_axis=0, concat_axis=1, tiled=True)  36.7 us
  transfers between devices with their start and end apart: 1, of which 1 were waited for; matrix products, arithmetic and copies ran while one was open for 0% of the time, Pallas kernels for 0%

commit v1 on v0

v1 whole, which is shorter than its diff:
```python
import functools

import jax
import jax.numpy as jnp
from jax import lax
from jax.experimental import pallas as pl
from jax.experimental.pallas import tpu as pltpu
from jax.sharding import PartitionSpec as P

MESH = pl.DeviceIdType.MESH
BLK = 128
NY = 4


def gram_body(cfg, tt_ref, ft_ref, out_ref, tb, pf, sb, xb, gp, rc, hb, rx, zb, rz, gf,
              ld_sem, sa_sem, ra_sem, sc_sem, rc_sem, sx_sem, rx_sem, sz_sem, rz_sem, sg_sem, rg_sem):
    nx, ny, nz, jl, scale = cfg
    half = gp.shape[0] // 2
    nq = nx * ny
    rows = half // nq
    g = lax.axis_index("grp")
    d = lax.axis_index("dev")
    x, c = g // 2, g % 2
    y, z = d // nz, d % nz
    q_own = x * ny + y

    def dev_id(gg, dd):
        return {"grp": gg, "dev": dd}

    chunks = []
    for t in range(ny):
        cg = (y + 1 + t) % ny
        cp = pltpu.make_async_copy(tt_ref.at[:, pl.ds(pl.multiple_of(cg * BLK, BLK), BLK), :], tb.at[t], ld_sem.at[t])
        cp.start()
        chunks.append(cp)

    barrier = pltpu.get_barrier_semaphore()
    nbar = 0

    def sig(gg, dd):
        pl.semaphore_signal(barrier, inc=1, device_id=dev_id(gg, dd), device_id_type=MESH)

    for k in range(1, ny * nz):
        sig(g, (d + k) % (ny * nz))
        nbar += 1
    for kx in range(1, nx):
        for ky in range(ny):
            sig(((x + kx) % nx) * 2 + c, ((y + ky) % ny) * nz + z)
            nbar += 1
    sig(x * 2 + 1 - c, d)
    nbar += 1

    zorder = sorted(range(nz), key=lambda k: (-min(k, nz - k), k))
    mine = pl.ds(pl.multiple_of(d * jl, jl), jl)
    jg = 256 // BLK
    sends = []
    for t in range(ny):
        chunks[t].wait()

        def proj(i, carry):
            rhs = tb[t, pl.ds(i * jg, jg)].reshape(jg * BLK, tb.shape[-1])
            o = lax.dot_general(ft_ref[...], rhs, (((1,), (1,)), ((), ())), preferred_element_type=jnp.float32)
            for rg in range(nz):
                for jj in range(jg):
                    pf[pl.ds(pl.multiple_of(rg * jl * 8 + (i * jg + jj) * 8, 8), 8), :] = o[rg * 8:(rg + 1) * 8, jj * BLK:(jj + 1) * BLK]
            return carry

        lax.fori_loop(0, jl // jg, proj, 0)
        cg = (y + 1 + t) % ny
        for n, zo in enumerate(zorder):
            rg = (z + zo) % nz
            local = t == ny - 1 and zo == 0
            for r in range(8):
                v = pf[pl.ds(pl.multiple_of(rg * jl * 8, 8) + r, jl, stride=8), :].astype(jnp.bfloat16)
                if local:
                    xb[mine, r * BLK:(r + 1) * BLK] = v
                else:
                    sb[t, n, :, r * BLK:(r + 1) * BLK] = v
            if t == 0 and n == 0:
                pl.semaphore_wait(barrier, nbar)
            if not local:
                cp = pltpu.make_async_remote_copy(sb.at[t, n], xb.at[mine, :], sa_sem.at[t, n], ra_sem.at[d],
                                                  device_id=dev_id(g, cg * nz + rg), device_id_type=MESH)
                cp.start()
                sends.append(cp)

    def wait_src(k, carry):
        src = (d + k) % (ny * nz)
        blk = xb.at[pl.ds(pl.multiple_of(src * jl, jl), jl), :]
        pltpu.make_async_copy(blk, blk, ra_sem.at[src]).wait()
        return carry

    lax.fori_loop(1, ny * nz, wait_src, 0)

    def gram_block(k, carry):
        idx = (k + 5 * (1 - c)) % 10
        a = (idx + 4) // 8 + (idx + 1) // 8 + (idx + 1) // 10
        b = idx - (a * 4 - a * (a - 1) // 2) + a
        xa = xb[pl.ds(pl.multiple_of(a * BLK, BLK), BLK), :]
        xc = xb[pl.ds(pl.multiple_of(b * BLK, BLK), BLK), :]
        o = lax.dot_general(xa, xc, (((1,), (1,)), ((), ())), preferred_element_type=jnp.float32)
        gp[pl.ds(pl.multiple_of(idx * BLK, BLK), BLK), :] = o * scale
        return carry

    lax.fori_loop(0, 5, gram_block, 0)
    own = pl.multiple_of(c * half, 8)
    other = pl.multiple_of((1 - c) * half, 8)
    core_cp = pltpu.make_async_remote_copy(gp.at[pl.ds(other, half), :], rc, sc_sem.at[0], rc_sem.at[0],
                                           device_id=dev_id(x * 2 + 1 - c, d), device_id_type=MESH)
    core_cp.start()
    lax.fori_loop(5, 10, gram_block, 0)
    core_cp.wait_recv()
    hb[...] = gp[pl.ds(own, half), :] + rc[...]

    xy_cps = []
    for kx in range(nx):
        for ky in range(ny):
            if kx == 0 and ky == 0:
                continue
            px, py = (x + kx) % nx, (y + ky) % ny
            q = px * ny + py
            cp = pltpu.make_async_remote_copy(hb.at[pl.ds(pl.multiple_of(q * rows, 8), rows), :], rx.at[q_own],
                                              sx_sem.at[0, kx * ny + ky], rx_sem.at[0, q_own],
                                              device_id=dev_id(px * 2 + c, py * nz + z), device_id_type=MESH)
            cp.start()
            xy_cps.append(cp)
    rx[q_own] = hb[pl.ds(pl.multiple_of(q_own * rows, 8), rows), :]

    def wait_xy(k, carry):
        q = (q_own + k) % nq
        pltpu.make_async_copy(rx.at[q], rx.at[q], rx_sem.at[0, q]).wait()
        return carry

    lax.fori_loop(1, nq, wait_xy, 0)
    acc = rx[0]
    for q in range(1, nq):
        acc += rx[q]
    zb[...] = acc

    z_cps = []
    for kz in range(1, nz):
        pz = (z + kz) % nz
        cp = pltpu.make_async_remote_copy(zb, rz.at[z], sz_sem.at[kz], rz_sem.at[z],
                                          device_id=dev_id(g, y * nz + pz), device_id_type=MESH)
        cp.start()
        z_cps.append(cp)
    rz[z] = acc
    for kz in range(1, nz):
        pz = (z + kz) % nz
        pltpu.make_async_copy(rz.at[pz], rz.at[pz], rz_sem.at[pz]).wait()
    acc = rz[0]
    for k in range(1, nz):
        acc += rz[k]

    here = pl.ds(pl.multiple_of(own + q_own * rows, 8), rows)
    gf[here, :] = acc
    ag_cps = []
    for kx in range(nx):
        for ky in range(ny):
            if kx == 0 and ky == 0:
                continue
            px, py = (x + kx) % nx, (y + ky) % ny
            cp = pltpu.make_async_remote_copy(gf.at[here, :], gf.at[here, :],
                                              sx_sem.at[1, kx * ny + ky], rx_sem.at[1, q_own],
                                              device_id=dev_id(px * 2 + c, py * nz + z), device_id_type=MESH)
            cp.start()
            ag_cps.append(cp)

    def wait_ag(k, carry):
        q = (q_own + k) % nq
        r = gf.at[pl.ds(pl.multiple_of(own + q * rows, 8), rows), :]
        pltpu.make_async_copy(r, r, rx_sem.at[1, q]).wait()
        return carry

    lax.fori_loop(1, nq, wait_ag, 0)
    mine_half = gf.at[pl.ds(own, half), :]
    fin = pltpu.make_async_remote_copy(mine_half, mine_half, sg_sem.at[0], rg_sem.at[0],
                                       device_id=dev_id(x * 2 + 1 - c, d), device_id_type=MESH)
    fin.start()
    oth = gf.at[pl.ds(other, half), :]
    pltpu.make_async_copy(oth, oth, rg_sem.at[0]).wait()
    idx = 0
    for a in range(4):
        for b in range(a, 4):
            out_ref[b * BLK:(b + 1) * BLK, a * BLK:(a + 1) * BLK] = gf[idx * BLK:(idx + 1) * BLK, :].T
            if a != b:
                out_ref[a * BLK:(a + 1) * BLK, b * BLK:(b + 1) * BLK] = jnp.zeros((BLK, BLK), jnp.float32)
            idx += 1
    fin.wait_send()
    core_cp.wait_send()
    for cp in sends + xy_cps + z_cps + ag_cps:
        cp.wait_send()


def gram_total(tt, ft, nx, ny, nz, scale):
    jl, ks, ni = tt.shape
    n2 = jl * ny * nz
    nq = nx * ny
    half = 5 * BLK
    rows = half // nq
    cfg = (nx, ny, nz, jl, scale)
    f32, bf16 = jnp.float32, jnp.bfloat16
    dma = pltpu.SemaphoreType.DMA
    return pl.pallas_call(
        functools.partial(gram_body, cfg),
        out_shape=jax.ShapeDtypeStruct((n2, n2), f32),
        in_specs=[pl.BlockSpec(memory_space=pl.ANY), pl.BlockSpec(memory_space=pltpu.VMEM)],
        out_specs=pl.BlockSpec(memory_space=pltpu.VMEM),
        scratch_shapes=[
            pltpu.VMEM((ny, jl, BLK, ni), bf16),
            pltpu.VMEM((nz * jl * 8, BLK), f32),
            pltpu.VMEM((ny, nz, jl, 8 * BLK), bf16),
            pltpu.VMEM((n2, 8 * BLK), bf16),
            pltpu.VMEM((2 * half, BLK), f32),
            pltpu.VMEM((half, BLK), f32),
            pltpu.VMEM((half, BLK), f32),
            pltpu.VMEM((nq, rows, BLK), f32),
            pltpu.VMEM((rows, BLK), f32),
            pltpu.VMEM((nz, rows, BLK), f32),
            pltpu.VMEM((2 * half, BLK), f32),
            dma((ny,)),
            dma((ny, nz)), dma((ny * nz,)),
            dma((1,)), dma((1,)),
            dma((2, nq)), dma((2, nq)),
            dma((nz,)), dma((nz,)),
            dma((1,)), dma((1,)),
        ],
        compiler_params=pltpu.CompilerParams(collective_id=0, has_side_effects=True, vmem_limit_bytes=48 << 20),
    )(tt, ft)


def own_block(full_tri):
    order = full_tri.shape[0]
    row_count = order // lax.axis_size("dev")
    col_count = order // lax.axis_size("grp")
    row_start = lax.axis_index("dev") * row_count
    col_start = lax.axis_index("grp") * col_count
    return lax.dynamic_slice(full_tri, (row_start, col_start), (row_count, col_count))


def per_device(ny, tensor_slab, mode_factor):
    ni, jl, kl, s = tensor_slab.shape
    grp, dev = lax.axis_size("grp"), lax.axis_size("dev")
    tt = jnp.transpose(tensor_slab, (1, 2, 3, 0)).reshape(jl, kl * s, ni)
    row_total = mode_factor.shape[1] * kl * s * grp
    gram = gram_total(tt, mode_factor.T, grp // 2, ny, dev // ny, 1.0 / row_total)
    return own_block(jnp.linalg.cholesky(gram, symmetrize_input=False).T)


def solution(mesh, ny=NY):
    in_specs = (P(None, "dev", "grp", None), P())
    out_specs = P("dev", "grp")
    return jax.shard_map(
        functools.partial(per_device, ny), mesh=mesh, in_specs=in_specs, out_specs=out_specs, check_vma=False
    )
```

time: 406 us -> 147 us (0.36)
  waiting for transfers between devices: 258 us -> 0 us
  Pallas kernels: 0 us -> 62 us
  blocking collectives: 36.7 us -> 0 us
  between operations: 16.1 us -> 2.78 us
  matrix products: 9.91 us -> 2.13 us
    psum x1 -> x0, waiting for transfers between devices: 258 us -> none  [per_device(): gram_total = lax.psum(gram_local, ('grp', 'dev'))]
    pallas_call x0 -> x1, Pallas kernels: none -> 62 us  [gram_total(): pl.pallas_call(functools.partial(gram_body, cfg), out_shape=jax.ShapeDtyp...]
    all_to_all x1 -> x0, blocking collectives: 36.7 us -> none  [per_device(): lax.all_to_all(projected, 'dev', split_axis=0, concat_axis=1, tiled=True)]
    dot_general x2 -> x0, matrix products: 7.77 us -> none  [the longest x1 6 us: per_device(): lax.dot_general(mode_factor, flat_slab, (((0,), (0,)), ((), ())), preferr...]
  transfers between devices with their start and end apart: 1 -> 0, of which waited for: 1 -> 0; matrix products, arithmetic and copies ran while one was open for 0% -> 0% of each run, Pallas kernels for 0% -> 0%
where the time goes in v1:
time: 147 us
  other arithmetic  78.6 us (53%)
  Pallas kernels  62 us (42%)
  between operations  2.78 us (2%)
  matrix products  2.13 us (1%)
  local copies, waits for them, and re-layouts  1.8 us (1%)
    another operation x14, other arithmetic, per_device(): return own_block(jnp.linalg.cholesky(gram, symmetrize_input=False).T)  78.6 us
    pallas_call x1, Pallas kernels, gram_total(): pl.pallas_call(functools.partial(gram_body, cfg), out_shape=jax.ShapeDtyp...  62 us

profile of v1, /device:TPU:1, one launch (start us, length us, event | category | flops | bytes accessed | tf_op | source)
XLA Modules:
  0.0 147.3 jit_solution(12860505772936717)
XLA Ops:
  0.0 0.0 copy-start
  0.0 0.8 copy-done
  0.8 62.0 %shard_map.28 = f32[512,512]{1,0:T(8,128)S(1)} custom-call(bf16[16,512,512]{2,1,0:T(8,128)(2,1)} %bitcast.23, bf16[64,512]{1,0:T(8,128)(2,1)S(1)} %bitcast.22), custom_call_target="tpu_custom_call" | custom-call | tf_op jit(solution)/shard_map/pallas_call | solution.py:204
  62.8 11.7 %cholesky.104 = f32[128,128]{1,0:T(8,128)S(1)} custom-call(f32[128,128]{1,0:T(8,128)S(1)} %cholesky.103), custom_call_target="Cholesky" | custom-call | tf_op jit(solution)/shard_map/jit(cholesky)/cholesky | solution.py:247
  74.6 9.8 %custom-call.27 = f32[1,128,128]{1,2,0:T(8,128)S(1)} custom-call(f32[1,128,128]{2,1,0:T(8,128)S(1)} %get-tuple-element.14), custom_call_target="InvertDiagBlocksLowerTriangular" | custom-call | tf_op jit(solution)/shard_map/jit(cholesky)/cholesky | solution.py:247
  84.4 0.4 fusion.2
  84.8 0.1 copy.3
  84.9 0.1 cholesky.224
  85.1 0.5 convolution_subtract_fusion
  85.6 11.7 %cholesky.217 = f32[128,128]{1,0:T(8,128)S(1)} custom-call(f32[128,128]{1,0:T(8,128)S(1)} %cholesky.267), custom_call_target="Cholesky" | custom-call | tf_op jit(solution)/shard_map/jit(cholesky)/cholesky | solution.py:247
  97.4 0.7 compare_reduce_fusion.2
  99.4 9.9 %custom-call.28 = f32[1,128,128]{1,2,0:T(8,128)S(1)} custom-call(f32[1,128,128]{2,1,0:T(8,128)S(1)} %get-tuple-element.11), custom_call_target="InvertDiagBlocksLowerTriangular" | custom-call | tf_op jit(solution)/shard_map/jit(cholesky)/cholesky | solution.py:247
  109.4 0.3 convolution_dynamic-update-slice_fusion
  109.6 0.4 convolution_subtract_fusion.1
  110.0 11.7 %cholesky.238 = f32[128,128]{1,0:T(8,128)S(1)} custom-call(f32[128,128]{1,0:T(8,128)S(1)} %cholesky.271), custom_call_target="Cholesky" | custom-call | tf_op jit(solution)/shard_map/jit(cholesky)/cholesky | solution.py:247
  121.8 0.6 compare_reduce_fusion.1
  123.1 9.8 %custom-call.29 = f32[1,128,128]{1,2,0:T(8,128)S(1)} custom-call(f32[1,128,128]{2,1,0:T(8,128)S(1)} %get-tuple-element.8), custom_call_target="InvertDiagBlocksLowerTriangular" | custom-call | tf_op jit(solution)/shard_map/jit(cholesky)/cholesky | solution.py:247
  132.9 0.2 convolution_dynamic-update-slice_fusion.1
  133.1 0.4 convolution_subtract_fusion.2
  133.5 11.7 %cholesky.255 = f32[128,128]{1,0:T(8,128)S(1)} custom-call(f32[128,128]{1,0:T(8,128)S(1)} %convolution_subtract_fusion.2), custom_call_target="Cholesky" | custom-call | tf_op jit(solution)/shard_map/jit(cholesky)/cholesky | solution.py:247
  145.2 0.6 compare_reduce_fusion
  146.5 0.1 fusion.12
  146.6 0.7 copy.6
  (8 shorter events, 0.2 us)
Async XLA Ops:
  0.0 0.8 copy-start

commit v2 on v1

--- a/solution.py
+++ b/solution.py
@@ -10,9 +10,119 @@
 MESH = pl.DeviceIdType.MESH
 BLK = 128
 NY = 4
-
-
-def gram_body(cfg, tt_ref, ft_ref, out_ref, tb, pf, sb, xb, gp, rc, hb, rx, zb, rz, gf,
+SUB = 16
+
+
+def split3(v):
+    hi = v.astype(jnp.bfloat16)
+    rest = v - hi.astype(jnp.float32)
+    mid = rest.astype(jnp.bfloat16)
+    low = (rest - mid.astype(jnp.float32)).astype(jnp.bfloat16)
+    return hi, mid, low
+
+
+def gram_like(a, b):
+    ah, am, al = split3(a)
+    bh, bm, bl = split3(b)
+    lhs = jnp.concatenate([ah, ah, am, ah, am, al], axis=0)
+    rhs = jnp.concatenate([bh, bm, bh, bl, bm, bh], axis=0)
+    return lax.dot_general(lhs, rhs, (((0,), (0,)), ((), ())), preferred_element_type=jnp.float32)
+
+
+def spread(v, q):
+    return jnp.broadcast_to(v[q:q + 1, :], (8, BLK))
+
+
+def factor_rows(rows, left):
+    sub = lax.broadcasted_iota(jnp.int32, (8, BLK), 0)
+    low, high = [], []
+    for q in range(SUB):
+        lane = left + q
+        low.append(jnp.broadcast_to(rows[0][0][:, lane:lane + 1], (8, BLK)) if q < 8 else None)
+        high.append(jnp.broadcast_to(rows[0][1][:, lane:lane + 1], (8, BLK)))
+    rows = [list(r) for r in rows]
+    piv = [jnp.ones((8, BLK), jnp.float32)] * 2
+
+    def at(q, p):
+        return spread(low[q], p) if p < 8 else spread(high[q], p - 8)
+
+    d = at(0, 0)
+    for q in range(SUB):
+        r = 1.0 / d
+        piv[q // 8] = jnp.where(sub == q % 8, d, piv[q // 8])
+        if q == SUB - 1:
+            break
+        e = at(q, q + 1)
+        d = at(q + 1, q + 1) - (e * e) * r
+        m_low = low[q] * r if q < 7 else None
+        m_high = high[q] * r
+        for p in range(q + 1, SUB):
+            e = at(q, p)
+            if p < 8:
+                low[p] = low[p] - m_low * e
+            high[p] = high[p] - m_high * e
+        k_low = jnp.where(sub > q, m_low, 0.0) if q < 7 else None
+        k_high = m_high if q < 8 else jnp.where(sub > q - 8, m_high, 0.0)
+        for t in rows:
+            e = spread(t[q // 8], q % 8)
+            if q < 7:
+                t[0] = t[0] - k_low * e
+            t[1] = t[1] - k_high * e
+    s0, s1 = lax.rsqrt(piv[0]), lax.rsqrt(piv[1])
+    return [jnp.concatenate([t[0] * s0, t[1] * s1], axis=0) for t in rows]
+
+
+def block_at(a, b):
+    return a * 4 - a * (a - 1) // 2 + b - a
+
+
+def cholesky_packed(g, inv):
+    n = 4
+    for k in range(n):
+        base = block_at(k, k) * BLK
+        last = k == n - 1
+        if not last:
+            inv[...] = (lax.broadcasted_iota(jnp.int32, (BLK, BLK), 0) == lax.broadcasted_iota(jnp.int32, (BLK, BLK), 1)).astype(jnp.float32)
+        refs = [(g, base)] if last else [(g, base), (inv, 0)]
+        for s in range(BLK // SUB):
+            at = s * SUB
+            tiles = [(r[o + at:o + at + 8, :], r[o + at + 8:o + at + SUB, :]) for r, o in refs]
+            done = factor_rows(tiles, at)
+            for (r, o), v in zip(refs, done):
+                r[o + at:o + at + SUB, :] = v
+            end = at + SUB
+            if end < BLK:
+                both = done[0] if last else jnp.concatenate(done, axis=1)
+                upd = gram_like(done[0], both)
+                for i, (r, o) in enumerate(refs):
+                    r[o + end:o + BLK, :] = r[o + end:o + BLK, :] - upd[end:, i * BLK:(i + 1) * BLK]
+        if last:
+            break
+        row = []
+        for b in range(k + 1, n):
+            o = block_at(k, b) * BLK
+            u = lax.dot_general(inv[...], g[o:o + BLK, :], (((1,), (0,)), ((), ())), precision=lax.Precision.HIGHEST, preferred_element_type=jnp.float32)
+            g[o:o + BLK, :] = u
+            row.append(u)
+        for a in range(k + 1, n):
+            for b in range(a, n):
+                o = block_at(a, b) * BLK
+                g[o:o + BLK, :] = g[o:o + BLK, :] - gram_like(row[a - k - 1], row[b - k - 1])
+
+
+def own_part(g, row, col):
+    a, b = row // 8, col // 2
+    o = pl.multiple_of(block_at(a, b) * BLK + (row % 8) * 16, 16)
+    v = g[pl.ds(o, 16), :]
+    shifted = jnp.concatenate([v[:, 64:], v[:, :64]], axis=1)
+    i = row * 16 + lax.broadcasted_iota(jnp.int32, (16, BLK), 0)
+    j = col * 64 + lax.broadcasted_iota(jnp.int32, (16, BLK), 1)
+    half = lax.broadcasted_iota(jnp.int32, (16, BLK), 1) * 0 + col % 2
+    v = jnp.where(half == 1, shifted, v)
+    return jnp.where(j >= i, v, 0.0)[:, :64]
+
+
+def gram_body(cfg, tt_ref, ft_ref, out_ref, tb, pf, sb, xb, gp, rc, hb, rx, zb, rz, gf, inv,
               ld_sem, sa_sem, ra_sem, sc_sem, rc_sem, sx_sem, rx_sem, sz_sem, rz_sem, sg_sem, rg_sem):
     nx, ny, nz, jl, scale = cfg
     half = gp.shape[0] // 2
@@ -179,20 +289,15 @@
     fin.start()
     oth = gf.at[pl.ds(other, half), :]
     pltpu.make_async_copy(oth, oth, rg_sem.at[0]).wait()
-    idx = 0
-    for a in range(4):
-        for b in range(a, 4):
-            out_ref[b * BLK:(b + 1) * BLK, a * BLK:(a + 1) * BLK] = gf[idx * BLK:(idx + 1) * BLK, :].T
-            if a != b:
-                out_ref[a * BLK:(a + 1) * BLK, b * BLK:(b + 1) * BLK] = jnp.zeros((BLK, BLK), jnp.float32)
-            idx += 1
     fin.wait_send()
     core_cp.wait_send()
     for cp in sends + xy_cps + z_cps + ag_cps:
         cp.wait_send()
-
-
-def gram_total(tt, ft, nx, ny, nz, scale):
+    cholesky_packed(gf, inv)
+    out_ref[...] = own_part(gf, d, g)
+
+
+def triangle(tt, ft, nx, ny, nz, scale):
     jl, ks, ni = tt.shape
     n2 = jl * ny * nz
     nq = nx * ny
@@ -203,7 +308,7 @@
     dma = pltpu.SemaphoreType.DMA
     return pl.pallas_call(
         functools.partial(gram_body, cfg),
-        out_shape=jax.ShapeDtypeStruct((n2, n2), f32),
+        out_shape=jax.ShapeDtypeStruct((n2 // (ny * nz), n2 // (2 * nx)), f32),
         in_specs=[pl.BlockSpec(memory_space=pl.ANY), pl.BlockSpec(memory_space=pltpu.VMEM)],
         out_specs=pl.BlockSpec(memory_space=pltpu.VMEM),
         scratch_shapes=[
@@ -218,6 +323,7 @@
             pltpu.VMEM((rows, BLK), f32),
             pltpu.VMEM((nz, rows, BLK), f32),
             pltpu.VMEM((2 * half, BLK), f32),
+            pltpu.VMEM((BLK, BLK), f32),
             dma((ny,)),
             dma((ny, nz)), dma((ny * nz,)),
             dma((1,)), dma((1,)),
@@ -229,22 +335,12 @@
     )(tt, ft)
 
 
-def own_block(full_tri):
-    order = full_tri.shape[0]
-    row_count = order // lax.axis_size("dev")
-    col_count = order // lax.axis_size("grp")
-    row_start = lax.axis_index("dev") * row_count
-    col_start = lax.axis_index("grp") * col_count
-    return lax.dynamic_slice(full_tri, (row_start, col_start), (row_count, col_count))
-
-
 def per_device(ny, tensor_slab, mode_factor):
     ni, jl, kl, s = tensor_slab.shape
     grp, dev = lax.axis_size("grp"), lax.axis_size("dev")
     tt = jnp.transpose(tensor_slab, (1, 2, 3, 0)).reshape(jl, kl * s, ni)
     row_total = mode_factor.shape[1] * kl * s * grp
-    gram = gram_total(tt, mode_factor.T, grp // 2, ny, dev // ny, 1.0 / row_total)
-    return own_block(jnp.linalg.cholesky(gram, symmetrize_input=False).T)
+    return triangle(tt, mode_factor.T, grp // 2, ny, dev // ny, 1.0 / row_total)
 
 
 def solution(mesh, ny=NY):

time: 147 us -> 77.5 us (0.53)
  other arithmetic: 78.6 us -> 0 us
  Pallas kernels: 62 us -> 76 us
  between operations: 2.78 us -> 0.01 us
  matrix products: 2.13 us -> 0 us
    another operation x14 -> x0, other arithmetic: 78.6 us -> none  [per_device(): return own_block(jnp.linalg.cholesky(gram, symmetrize_input=False).T)]
    pallas_call x1, Pallas kernels: 62 us -> 76 us  [triangle(): pl.pallas_call(functools.partial(gram_body, cfg), out_shape=jax.ShapeDtyp...]
    another operation x6 -> x0, matrix products: 2.13 us -> none  [per_device(): return own_block(jnp.linalg.cholesky(gram, symmetrize_input=False).T)]
where the time goes in v2:
time: 77.5 us; the launch traced here: 77.4 us
  Pallas kernels  76 us (98%)
  local copies, waits for them, and re-layouts  1.44 us (2%)
    pallas_call x1, Pallas kernels, triangle(): pl.pallas_call(functools.partial(gram_body, cfg), out_shape=jax.ShapeDtyp...  76 us

profile of v2, /device:TPU:1, one launch (start us, length us, event | category | flops | bytes accessed | tf_op | source)
XLA Modules:
  0.0 77.4 jit_solution(15050419060965971712)
XLA Ops:
  0.0 0.0 copy-start
  0.0 0.8 %copy-done = bf16[512,64]{0,1:T(8,128)(2,1)S(1)} copy-done((bf16[512,64]{0,1:T(8,128)(2,1)S(1)}, bf16[512,64]{0,1:T(8,128)(2,1)}, u32[]{:S(2)}) %copy-start) | copy-done | bytes 65560
  0.8 76.0 %shard_map.28 = f32[16,64]{1,0:T(8,128)S(1)} custom-call(bf16[16,512,512]{2,1,0:T(8,128)(2,1)} %bitcast.5, bf16[64,512]{1,0:T(8,128)(2,1)S(1)} %bitcast.4), custom_call_target="tpu_custom_call" | custom-call | tf_op jit(solution)/shard_map/pallas_call | solution.py:309
  76.8 0.6 copy.4
Async XLA Ops:
  0.0 0.8 %copy-start = (bf16[512,64]{0,1:T(8,128)(2,1)S(1)}, bf16[512,64]{0,1:T(8,128)(2,1)}, u32[]{:S(2)}) copy-start(bf16[512,64]{0,1:T(8,128)(2,1)} %param.3) | copy-start | bytes 196612

commit v3 on v2

--- a/solution.py
+++ b/solution.py
@@ -11,6 +11,7 @@
 BLK = 128
 NY = 4
 SUB = 16
+STRIP = 32
 
 
 def split3(v):
@@ -33,43 +34,46 @@
     return jnp.broadcast_to(v[q:q + 1, :], (8, BLK))
 
 
-def factor_rows(rows, left):
+def eliminate(rows, left, first):
     sub = lax.broadcasted_iota(jnp.int32, (8, BLK), 0)
-    low, high = [], []
-    for q in range(SUB):
-        lane = left + q
-        low.append(jnp.broadcast_to(rows[0][0][:, lane:lane + 1], (8, BLK)) if q < 8 else None)
-        high.append(jnp.broadcast_to(rows[0][1][:, lane:lane + 1], (8, BLK)))
-    rows = [list(r) for r in rows]
+    pieces = range(first, len(rows[0]))
+    col = [{i: jnp.broadcast_to(rows[0][i][:, left + q:left + q + 1], (8, BLK)) for i in pieces if i > first or q < 8}
+           for q in range(SUB)]
     piv = [jnp.ones((8, BLK), jnp.float32)] * 2
 
     def at(q, p):
-        return spread(low[q], p) if p < 8 else spread(high[q], p - 8)
+        return spread(col[q][first + p // 8], p % 8)
 
     d = at(0, 0)
     for q in range(SUB):
         r = 1.0 / d
         piv[q // 8] = jnp.where(sub == q % 8, d, piv[q // 8])
-        if q == SUB - 1:
-            break
-        e = at(q, q + 1)
-        d = at(q + 1, q + 1) - (e * e) * r
-        m_low = low[q] * r if q < 7 else None
-        m_high = high[q] * r
+        if q < SUB - 1:
+            e = at(q, q + 1)
+            d = at(q + 1, q + 1) - (e * e) * r
+        mult = {i: v * r for i, v in col[q].items() if i >= first + q // 8}
         for p in range(q + 1, SUB):
             e = at(q, p)
-            if p < 8:
-                low[p] = low[p] - m_low * e
-            high[p] = high[p] - m_high * e
-        k_low = jnp.where(sub > q, m_low, 0.0) if q < 7 else None
-        k_high = m_high if q < 8 else jnp.where(sub > q - 8, m_high, 0.0)
+            for i in col[p]:
+                if i >= first + p // 8:
+                    col[p][i] = col[p][i] - mult[i] * e
+        here = first + q // 8
         for t in rows:
-            e = spread(t[q // 8], q % 8)
-            if q < 7:
-                t[0] = t[0] - k_low * e
-            t[1] = t[1] - k_high * e
-    s0, s1 = lax.rsqrt(piv[0]), lax.rsqrt(piv[1])
-    return [jnp.concatenate([t[0] * s0, t[1] * s1], axis=0) for t in rows]
+            e = spread(t[here], q % 8)
+            for i in mult:
+                if i > here:
+                    t[i] = t[i] - mult[i] * e
+                elif q % 8 < 7:
+                    t[i] = t[i] - jnp.where(sub > q % 8, mult[i], 0.0) * e
+    return [lax.rsqrt(v) for v in piv]
+
+
+def factor_rows(rows, left):
+    rows = [list(t) for t in rows]
+    scales = []
+    for first in range(0, len(rows[0]), 2):
+        scales += eliminate(rows, left + first * 8, first)
+    return [jnp.concatenate([v * s for v, s in zip(t, scales)], axis=0) for t in rows]
 
 
 def block_at(a, b):
@@ -84,13 +88,13 @@
         if not last:
             inv[...] = (lax.broadcasted_iota(jnp.int32, (BLK, BLK), 0) == lax.broadcasted_iota(jnp.int32, (BLK, BLK), 1)).astype(jnp.float32)
         refs = [(g, base)] if last else [(g, base), (inv, 0)]
-        for s in range(BLK // SUB):
-            at = s * SUB
-            tiles = [(r[o + at:o + at + 8, :], r[o + at + 8:o + at + SUB, :]) for r, o in refs]
+        for s in range(BLK // STRIP):
+            at = s * STRIP
+            tiles = [[r[o + at + i:o + at + i + 8, :] for i in range(0, STRIP, 8)] for r, o in refs]
             done = factor_rows(tiles, at)
             for (r, o), v in zip(refs, done):
-                r[o + at:o + at + SUB, :] = v
-            end = at + SUB
+                r[o + at:o + at + STRIP, :] = v
+            end = at + STRIP
             if end < BLK:
                 both = done[0] if last else jnp.concatenate(done, axis=1)
                 upd = gram_like(done[0], both)
@@ -122,8 +126,8 @@
     return jnp.where(j >= i, v, 0.0)[:, :64]
 
 
-def gram_body(cfg, tt_ref, ft_ref, out_ref, tb, pf, sb, xb, gp, rc, hb, rx, zb, rz, gf, inv,
-              ld_sem, sa_sem, ra_sem, sc_sem, rc_sem, sx_sem, rx_sem, sz_sem, rz_sem, sg_sem, rg_sem):
+def gram_body(cfg, tt_ref, ft_any, out_ref, ft_ref, tb, pf, sb, xb, gp, rc, hb, rx, zb, rz, gf, inv,
+              ld_sem, sa_sem, ra_sem, sc_sem, rc_sem, sx_sem, rx_sem, sz_sem, rz_sem, sg_sem, rg_sem, ft_sem):
     nx, ny, nz, jl, scale = cfg
     half = gp.shape[0] // 2
     nq = nx * ny
@@ -137,6 +141,8 @@
     def dev_id(gg, dd):
         return {"grp": gg, "dev": dd}
 
+    ft_cp = pltpu.make_async_copy(ft_any, ft_ref, ft_sem)
+    ft_cp.start()
     chunks = []
     for t in range(ny):
         cg = (y + 1 + t) % ny
@@ -164,6 +170,7 @@
     mine = pl.ds(pl.multiple_of(d * jl, jl), jl)
     jg = 256 // BLK
     sends = []
+    ft_cp.wait()
     for t in range(ny):
         chunks[t].wait()
 
@@ -222,6 +229,7 @@
     core_cp.wait_recv()
     hb[...] = gp[pl.ds(own, half), :] + rc[...]
 
+    plane = sorted(((kx, ky) for kx in range(nx) for ky in range(ny)), key=lambda k: min(k[0], nx - k[0]) + min(k[1], ny - k[1]))
     xy_cps = []
     for kx in range(nx):
         for ky in range(ny):
@@ -276,22 +284,21 @@
             cp.start()
             ag_cps.append(cp)
 
-    def wait_ag(k, carry):
-        q = (q_own + k) % nq
-        r = gf.at[pl.ds(pl.multiple_of(own + q * rows, 8), rows), :]
-        pltpu.make_async_copy(r, r, rx_sem.at[1, q]).wait()
-        return carry
-
-    lax.fori_loop(1, nq, wait_ag, 0)
-    mine_half = gf.at[pl.ds(own, half), :]
-    fin = pltpu.make_async_remote_copy(mine_half, mine_half, sg_sem.at[0], rg_sem.at[0],
-                                       device_id=dev_id(x * 2 + 1 - c, d), device_id_type=MESH)
-    fin.start()
-    oth = gf.at[pl.ds(other, half), :]
-    pltpu.make_async_copy(oth, oth, rg_sem.at[0]).wait()
-    fin.wait_send()
+    forward = []
+    for kx, ky in plane:
+        q = ((x + kx) % nx) * ny + (y + ky) % ny
+        piece = gf.at[pl.ds(pl.multiple_of(own + q * rows, 8), rows), :]
+        if (kx, ky) != (0, 0):
+            pltpu.make_async_copy(piece, piece, rx_sem.at[1, q]).wait()
+        cp = pltpu.make_async_remote_copy(piece, piece, sg_sem.at[q], rg_sem.at[q],
+                                          device_id=dev_id(x * 2 + 1 - c, d), device_id_type=MESH)
+        cp.start()
+        forward.append(cp)
+    for q in range(nq):
+        piece = gf.at[pl.ds(pl.multiple_of(other + q * rows, 8), rows), :]
+        pltpu.make_async_copy(piece, piece, rg_sem.at[q]).wait()
     core_cp.wait_send()
-    for cp in sends + xy_cps + z_cps + ag_cps:
+    for cp in sends + xy_cps + z_cps + ag_cps + forward:
         cp.wait_send()
     cholesky_packed(gf, inv)
     out_ref[...] = own_part(gf, d, g)
@@ -309,9 +316,10 @@
     return pl.pallas_call(
         functools.partial(gram_body, cfg),
         out_shape=jax.ShapeDtypeStruct((n2 // (ny * nz), n2 // (2 * nx)), f32),
-        in_specs=[pl.BlockSpec(memory_space=pl.ANY), pl.BlockSpec(memory_space=pltpu.VMEM)],
+        in_specs=[pl.BlockSpec(memory_space=pl.ANY)] * 2,
         out_specs=pl.BlockSpec(memory_space=pltpu.VMEM),
         scratch_shapes=[
+            pltpu.VMEM(ft.shape, bf16),
             pltpu.VMEM((ny, jl, BLK, ni), bf16),
             pltpu.VMEM((nz * jl * 8, BLK), f32),
             pltpu.VMEM((ny, nz, jl, 8 * BLK), bf16),
@@ -329,7 +337,8 @@
             dma((1,)), dma((1,)),
             dma((2, nq)), dma((2, nq)),
             dma((nz,)), dma((nz,)),
-            dma((1,)), dma((1,)),
+            dma((nq,)), dma((nq,)),
+            dma(()),
         ],
         compiler_params=pltpu.CompilerParams(collective_id=0, has_side_effects=True, vmem_limit_bytes=48 << 20),
     )(tt, ft)

time: 77.5 us -> 75.9 us (0.979)
  Pallas kernels: 76 us -> 74.3 us
    pallas_call x1, Pallas kernels: 76 us -> 74.3 us  [triangle(): pl.pallas_call(functools.partial(gram_body, cfg), out_shape=jax.ShapeDtyp...]
where the time goes in v3:
time: 75.9 us; the launch traced here: 75.8 us
  Pallas kernels  74.3 us (98%)
  local copies, waits for them, and re-layouts  1.44 us (2%)
    pallas_call x1, Pallas kernels, triangle(): pl.pallas_call(functools.partial(gram_body, cfg), out_shape=jax.ShapeDtyp...  74.3 us

profile of v3, /device:TPU:1, one launch (start us, length us, event | category | flops | bytes accessed | tf_op | source)
XLA Modules:
  0.0 75.8 jit_solution(17655463411850918822)
XLA Ops:
  0.0 0.0 copy-start
  0.0 0.8 %copy-done = bf16[512,64]{0,1:T(8,128)(2,1)S(1)} copy-done((bf16[512,64]{0,1:T(8,128)(2,1)S(1)}, bf16[512,64]{0,1:T(8,128)(2,1)}, u32[]{:S(2)}) %copy-start) | copy-done | bytes 65560
  0.8 74.3 %shard_map.28 = f32[16,64]{1,0:T(8,128)S(1)} custom-call(bf16[16,512,512]{2,1,0:T(8,128)(2,1)} %bitcast.5, bf16[64,512]{1,0:T(8,128)(2,1)S(1)} %bitcast.4), custom_call_target="tpu_custom_call" | custom-call | tf_op jit(solution)/shard_map/pallas_call | solution.py:316
  75.2 0.6 copy.4
Async XLA Ops:
  0.0 0.8 %copy-start = (bf16[512,64]{0,1:T(8,128)(2,1)S(1)}, bf16[512,64]{0,1:T(8,128)(2,1)}, u32[]{:S(2)}) copy-start(bf16[512,64]{0,1:T(8,128)(2,1)} %param.3) | copy-start | bytes 196612

commit v4 on v3

--- a/solution.py
+++ b/solution.py
@@ -126,10 +126,10 @@
     return jnp.where(j >= i, v, 0.0)[:, :64]
 
 
-def gram_body(cfg, tt_ref, ft_any, out_ref, ft_ref, tb, pf, sb, xb, gp, rc, hb, rx, zb, rz, gf, inv,
-              ld_sem, sa_sem, ra_sem, sc_sem, rc_sem, sx_sem, rx_sem, sz_sem, rz_sem, sg_sem, rg_sem, ft_sem):
+def gram_body(cfg, tt_ref, ft_any, out_ref, ft_ref, tb, pf, sb, xb, gp, rc, hb, rx, zb, rz, gf, work, inv,
+              ld_sem, sa_sem, ra_sem, sc_sem, rc_sem, sx_sem, rx_sem, sz_sem, rz_sem, sg_sem, rg_sem, ft_sem, col_sem):
     nx, ny, nz, jl, scale = cfg
-    half = gp.shape[0] // 2
+    half = gp.shape[1]
     nq = nx * ny
     rows = half // nq
     g = lax.axis_index("grp")
@@ -145,7 +145,7 @@
     ft_cp.start()
     chunks = []
     for t in range(ny):
-        cg = (y + 1 + t) % ny
+        cg = (y + t) % ny
         cp = pltpu.make_async_copy(tt_ref.at[:, pl.ds(pl.multiple_of(cg * BLK, BLK), BLK), :], tb.at[t], ld_sem.at[t])
         cp.start()
         chunks.append(cp)
@@ -156,13 +156,14 @@
     def sig(gg, dd):
         pl.semaphore_signal(barrier, inc=1, device_id=dev_id(gg, dd), device_id_type=MESH)
 
-    for k in range(1, ny * nz):
-        sig(g, (d + k) % (ny * nz))
+    for k in range(1, nz):
+        sig(g, y * nz + (z + k) % nz)
         nbar += 1
-    for kx in range(1, nx):
+    for kx in range(nx):
         for ky in range(ny):
-            sig(((x + kx) % nx) * 2 + c, ((y + ky) % ny) * nz + z)
-            nbar += 1
+            if (kx, ky) != (0, 0):
+                sig(((x + kx) % nx) * 2 + c, ((y + ky) % ny) * nz + z)
+                nbar += 1
     sig(x * 2 + 1 - c, d)
     nbar += 1
 
@@ -183,10 +184,10 @@
             return carry
 
         lax.fori_loop(0, jl // jg, proj, 0)
-        cg = (y + 1 + t) % ny
+        cg = (y + t) % ny
         for n, zo in enumerate(zorder):
             rg = (z + zo) % nz
-            local = t == ny - 1 and zo == 0
+            local = t == 0 and zo == 0
             for r in range(8):
                 v = pf[pl.ds(pl.multiple_of(rg * jl * 8, 8) + r, jl, stride=8), :].astype(jnp.bfloat16)
                 if local:
@@ -195,39 +196,53 @@
                     sb[t, n, :, r * BLK:(r + 1) * BLK] = v
             if t == 0 and n == 0:
                 pl.semaphore_wait(barrier, nbar)
+                for k in range(1, ny):
+                    pl.semaphore_signal(col_sem.at[k], inc=1, device_id=dev_id(g, (y + k) % ny * nz + z), device_id_type=MESH)
+            if t == 1 and n == 0:
+                for k in range(1, ny):
+                    pl.semaphore_wait(col_sem.at[k], 1)
             if not local:
                 cp = pltpu.make_async_remote_copy(sb.at[t, n], xb.at[mine, :], sa_sem.at[t, n], ra_sem.at[d],
                                                   device_id=dev_id(g, cg * nz + rg), device_id_type=MESH)
                 cp.start()
                 sends.append(cp)
 
-    def wait_src(k, carry):
-        src = (d + k) % (ny * nz)
-        blk = xb.at[pl.ds(pl.multiple_of(src * jl, jl), jl), :]
-        pltpu.make_async_copy(blk, blk, ra_sem.at[src]).wait()
-        return carry
-
-    lax.fori_loop(1, ny * nz, wait_src, 0)
-
-    def gram_block(k, carry):
-        idx = (k + 5 * (1 - c)) % 10
-        a = (idx + 4) // 8 + (idx + 1) // 8 + (idx + 1) // 10
-        b = idx - (a * 4 - a * (a - 1) // 2) + a
-        xa = xb[pl.ds(pl.multiple_of(a * BLK, BLK), BLK), :]
-        xc = xb[pl.ds(pl.multiple_of(b * BLK, BLK), BLK), :]
-        o = lax.dot_general(xa, xc, (((1,), (1,)), ((), ())), preferred_element_type=jnp.float32)
-        gp[pl.ds(pl.multiple_of(idx * BLK, BLK), BLK), :] = o * scale
-        return carry
-
-    lax.fori_loop(0, 5, gram_block, 0)
+    partner = dev_id(x * 2 + 1 - c, d)
+
+    def to_core(idx):
+        at = pl.ds(pl.multiple_of(idx * (BLK // 2), BLK // 2), BLK // 2)
+        return pltpu.make_async_remote_copy(gp.at[1 - c, at, :], rc.at[at, :], sc_sem.at[idx], rc_sem.at[idx],
+                                            device_id=partner, device_id_type=MESH)
+
+    for t in range(ny):
+        ya = (y + ny - t) % ny
+        for k in range(0 if t else 1, nz):
+            src = ya * nz + (z + k) % nz
+            landed = xb.at[pl.ds(pl.multiple_of(src * jl, jl), jl), :]
+            pltpu.make_async_copy(landed, landed, ra_sem.at[src]).wait()
+
+        def gram_block(u, carry, t=t):
+            a = (y + ny - t) % ny
+            b = (y + ny - u) % ny
+            less = (b - a + ny - 1) // ny
+            lo = b + (a - b) * less
+            hi = a + b - lo
+            idx = lo * 4 - lo * (lo - 1) // 2 + hi - lo
+            xa = xb[pl.ds(pl.multiple_of(lo * BLK, BLK), BLK), :]
+            xc = xb[pl.ds(pl.multiple_of(hi * BLK, BLK), BLK), :]
+            o = lax.dot_general(xa, xc, (((1,), (1,)), ((), ())), preferred_element_type=jnp.float32) * scale
+            at = pl.ds(pl.multiple_of(idx * (BLK // 2), BLK // 2), BLK // 2)
+            gp[0, at, :] = o[:BLK // 2]
+            gp[1, at, :] = o[BLK // 2:]
+            to_core(idx).start()
+            return carry
+
+        lax.fori_loop(0, t + 1, gram_block, 0)
     own = pl.multiple_of(c * half, 8)
     other = pl.multiple_of((1 - c) * half, 8)
-    core_cp = pltpu.make_async_remote_copy(gp.at[pl.ds(other, half), :], rc, sc_sem.at[0], rc_sem.at[0],
-                                           device_id=dev_id(x * 2 + 1 - c, d), device_id_type=MESH)
-    core_cp.start()
-    lax.fori_loop(5, 10, gram_block, 0)
-    core_cp.wait_recv()
-    hb[...] = gp[pl.ds(own, half), :] + rc[...]
+    for idx in range(10):
+        to_core(idx).wait_recv()
+    hb[...] = gp[c] + rc[...]
 
     plane = sorted(((kx, ky) for kx in range(nx) for ky in range(ny)), key=lambda k: min(k[0], nx - k[0]) + min(k[1], ny - k[1]))
     xy_cps = []
@@ -297,11 +312,16 @@
     for q in range(nq):
         piece = gf.at[pl.ds(pl.multiple_of(other + q * rows, 8), rows), :]
         pltpu.make_async_copy(piece, piece, rg_sem.at[q]).wait()
-    core_cp.wait_send()
+    hb_rows = BLK // 2
+    for idx in range(10):
+        for h in range(2):
+            work[idx * BLK + h * hb_rows:idx * BLK + (h + 1) * hb_rows, :] = gf[h * half + idx * hb_rows:h * half + (idx + 1) * hb_rows, :]
+    cholesky_packed(work, inv)
+    out_ref[...] = own_part(work, d, g)
+    for idx in range(10):
+        to_core(idx).wait_send()
     for cp in sends + xy_cps + z_cps + ag_cps + forward:
         cp.wait_send()
-    cholesky_packed(gf, inv)
-    out_ref[...] = own_part(gf, d, g)
 
 
 def triangle(tt, ft, nx, ny, nz, scale):
@@ -316,7 +336,7 @@
     return pl.pallas_call(
         functools.partial(gram_body, cfg),
         out_shape=jax.ShapeDtypeStruct((n2 // (ny * nz), n2 // (2 * nx)), f32),
-        in_specs=[pl.BlockSpec(memory_space=pl.ANY)] * 2,
+        in_specs=[pl.BlockSpec(memory_space=pltpu.MemorySpace.HBM)] * 2,
         out_specs=pl.BlockSpec(memory_space=pltpu.VMEM),
         scratch_shapes=[
             pltpu.VMEM(ft.shape, bf16),
@@ -324,21 +344,23 @@
             pltpu.VMEM((nz * jl * 8, BLK), f32),
             pltpu.VMEM((ny, nz, jl, 8 * BLK), bf16),
             pltpu.VMEM((n2, 8 * BLK), bf16),
-            pltpu.VMEM((2 * half, BLK), f32),
+            pltpu.VMEM((2, half, BLK), f32),
             pltpu.VMEM((half, BLK), f32),
             pltpu.VMEM((half, BLK), f32),
             pltpu.VMEM((nq, rows, BLK), f32),
             pltpu.VMEM((rows, BLK), f32),
             pltpu.VMEM((nz, rows, BLK), f32),
             pltpu.VMEM((2 * half, BLK), f32),
+            pltpu.VMEM((2 * half, BLK), f32),
             pltpu.VMEM((BLK, BLK), f32),
             dma((ny,)),
             dma((ny, nz)), dma((ny * nz,)),
-            dma((1,)), dma((1,)),
+            dma((10,)), dma((10,)),
             dma((2, nq)), dma((2, nq)),
             dma((nz,)), dma((nz,)),
             dma((nq,)), dma((nq,)),
             dma(()),
+            pltpu.SemaphoreType.REGULAR((ny,)),
         ],
         compiler_params=pltpu.CompilerParams(collective_id=0, has_side_effects=True, vmem_limit_bytes=48 << 20),
     )(tt, ft)

time: 75.9 us -> 75.3 us (level)
  no operation moved by 1% of the time
where the time goes in v4:
time: 75.3 us; the launch traced here: 75.2 us
  Pallas kernels  73.7 us (98%)
  local copies, waits for them, and re-layouts  1.44 us (2%)
    pallas_call x1, Pallas kernels, triangle(): pl.pallas_call(functools.partial(gram_body, cfg), out_shape=jax.ShapeDtyp...  73.7 us

profile of v4, /device:TPU:1, one launch (start us, length us, event | category | flops | bytes accessed | tf_op | source)
XLA Modules:
  0.0 75.2 jit_solution(13665606321979392367)
XLA Ops:
  0.0 0.0 copy-start
  0.0 0.8 %copy-done = bf16[512,64]{0,1:T(8,128)(2,1)S(1)} copy-done((bf16[512,64]{0,1:T(8,128)(2,1)S(1)}, bf16[512,64]{0,1:T(8,128)(2,1)}, u32[]{:S(2)}) %copy-start) | copy-done | bytes 65560
  0.8 73.7 %shard_map.28 = f32[16,64]{1,0:T(8,128)S(1)} custom-call(bf16[16,512,512]{2,1,0:T(8,128)(2,1)} %bitcast.5, bf16[64,512]{1,0:T(8,128)(2,1)S(1)} %bitcast.4), custom_call_target="tpu_custom_call" | custom-call | tf_op jit(solution)/shard_map/pallas_call | solution.py:336
  74.6 0.6 copy.4
Async XLA Ops:
  0.0 0.8 %copy-start = (bf16[512,64]{0,1:T(8,128)(2,1)S(1)}, bf16[512,64]{0,1:T(8,128)(2,1)}, u32[]{:S(2)}) copy-start(bf16[512,64]{0,1:T(8,128)(2,1)} %param.3) | copy-start | bytes 196612

commit v5 on v4

--- a/solution.py
+++ b/solution.py
@@ -12,6 +12,7 @@
 NY = 4
 SUB = 16
 STRIP = 32
+PARTS = (16, 24)
 
 
 def split3(v):
@@ -80,14 +81,32 @@
     return a * 4 - a * (a - 1) // 2 + b - a
 
 
+def product(a, b):
+    ah, am, al = split3(a)
+    bh, bm, bl = split3(b)
+    lhs = jnp.concatenate([ah, ah, am, ah, am, al], axis=1)
+    rhs = jnp.concatenate([bh, bm, bh, bl, bm, bh], axis=0)
+    return lax.dot_general(lhs, rhs, (((1,), (0,)), ((), ())), preferred_element_type=jnp.float32)
+
+
 def cholesky_packed(g, inv):
     n = 4
+    eye = (lax.broadcasted_iota(jnp.int32, (BLK, BLK), 0) == lax.broadcasted_iota(jnp.int32, (BLK, BLK), 1)).astype(jnp.float32)
+    def panel(k, b):
+        o = block_at(k, b) * BLK
+        g[o:o + BLK, :] = product(inv[k % 2], g[o:o + BLK, :])
+
+    def update(k, a, b):
+        o, oa, ob = (block_at(*ab) * BLK for ab in ((a, b), (k, a), (k, b)))
+        g[o:o + BLK, :] = g[o:o + BLK, :] - gram_like(g[oa:oa + BLK, :], g[ob:ob + BLK, :])
+
     for k in range(n):
         base = block_at(k, k) * BLK
         last = k == n - 1
+        way = inv.at[k % 2]
         if not last:
-            inv[...] = (lax.broadcasted_iota(jnp.int32, (BLK, BLK), 0) == lax.broadcasted_iota(jnp.int32, (BLK, BLK), 1)).astype(jnp.float32)
-        refs = [(g, base)] if last else [(g, base), (inv, 0)]
+            way[...] = eye
+        refs = [(g, base)] if last else [(g, base), (way, 0)]
         for s in range(BLK // STRIP):
             at = s * STRIP
             tiles = [[r[o + at + i:o + at + i + 8, :] for i in range(0, STRIP, 8)] for r, o in refs]
@@ -102,16 +121,11 @@
                     r[o + end:o + BLK, :] = r[o + end:o + BLK, :] - upd[end:, i * BLK:(i + 1) * BLK]
         if last:
             break
-        row = []
         for b in range(k + 1, n):
-            o = block_at(k, b) * BLK
-            u = lax.dot_general(inv[...], g[o:o + BLK, :], (((1,), (0,)), ((), ())), precision=lax.Precision.HIGHEST, preferred_element_type=jnp.float32)
-            g[o:o + BLK, :] = u
-            row.append(u)
+            panel(k, b)
         for a in range(k + 1, n):
             for b in range(a, n):
-                o = block_at(a, b) * BLK
-                g[o:o + BLK, :] = g[o:o + BLK, :] - gram_like(row[a - k - 1], row[b - k - 1])
+                update(k, a, b)
 
 
 def own_part(g, row, col):
@@ -245,73 +259,69 @@
     hb[...] = gp[c] + rc[...]
 
     plane = sorted(((kx, ky) for kx in range(nx) for ky in range(ny)), key=lambda k: min(k[0], nx - k[0]) + min(k[1], ny - k[1]))
-    xy_cps = []
-    for kx in range(nx):
-        for ky in range(ny):
-            if kx == 0 and ky == 0:
-                continue
-            px, py = (x + kx) % nx, (y + ky) % ny
-            q = px * ny + py
-            cp = pltpu.make_async_remote_copy(hb.at[pl.ds(pl.multiple_of(q * rows, 8), rows), :], rx.at[q_own],
-                                              sx_sem.at[0, kx * ny + ky], rx_sem.at[0, q_own],
-                                              device_id=dev_id(px * 2 + c, py * nz + z), device_id_type=MESH)
-            cp.start()
-            xy_cps.append(cp)
+    parts = []
+    at_row = 0
+    for n in PARTS:
+        parts.append((at_row, n))
+        at_row += n
+    later = []
+
+    def send(src, dst, s_sem, r_sem, to):
+        cp = pltpu.make_async_remote_copy(src, dst, s_sem, r_sem, device_id=to, device_id_type=MESH)
+        cp.start()
+        later.append(cp)
+
+    def at_peer(kx, ky):
+        px, py = (x + kx) % nx, (y + ky) % ny
+        return px * ny + py, dev_id(px * 2 + c, py * nz + z)
+
+    def held(base, r0, n):
+        return gf.at[pl.ds(pl.multiple_of(base + r0, 8), n), :]
+
+    for p, (r0, n) in enumerate(parts):
+        for kx, ky in plane[1:]:
+            q, to = at_peer(kx, ky)
+            send(hb.at[pl.ds(pl.multiple_of(q * rows + r0, 8), n), :], rx.at[q_own, pl.ds(r0, n)],
+                 sx_sem.at[0, p, kx * ny + ky], rx_sem.at[0, p, q_own], to)
     rx[q_own] = hb[pl.ds(pl.multiple_of(q_own * rows, 8), rows), :]
-
-    def wait_xy(k, carry):
-        q = (q_own + k) % nq
-        pltpu.make_async_copy(rx.at[q], rx.at[q], rx_sem.at[0, q]).wait()
-        return carry
-
-    lax.fori_loop(1, nq, wait_xy, 0)
-    acc = rx[0]
-    for q in range(1, nq):
-        acc += rx[q]
-    zb[...] = acc
-
-    z_cps = []
-    for kz in range(1, nz):
-        pz = (z + kz) % nz
-        cp = pltpu.make_async_remote_copy(zb, rz.at[z], sz_sem.at[kz], rz_sem.at[z],
-                                          device_id=dev_id(g, y * nz + pz), device_id_type=MESH)
-        cp.start()
-        z_cps.append(cp)
-    rz[z] = acc
-    for kz in range(1, nz):
-        pz = (z + kz) % nz
-        pltpu.make_async_copy(rz.at[pz], rz.at[pz], rz_sem.at[pz]).wait()
-    acc = rz[0]
-    for k in range(1, nz):
-        acc += rz[k]
-
-    here = pl.ds(pl.multiple_of(own + q_own * rows, 8), rows)
-    gf[here, :] = acc
-    ag_cps = []
-    for kx in range(nx):
-        for ky in range(ny):
-            if kx == 0 and ky == 0:
-                continue
-            px, py = (x + kx) % nx, (y + ky) % ny
-            cp = pltpu.make_async_remote_copy(gf.at[here, :], gf.at[here, :],
-                                              sx_sem.at[1, kx * ny + ky], rx_sem.at[1, q_own],
-                                              device_id=dev_id(px * 2 + c, py * nz + z), device_id_type=MESH)
-            cp.start()
-            ag_cps.append(cp)
-
-    forward = []
-    for kx, ky in plane:
-        q = ((x + kx) % nx) * ny + (y + ky) % ny
-        piece = gf.at[pl.ds(pl.multiple_of(own + q * rows, 8), rows), :]
-        if (kx, ky) != (0, 0):
-            pltpu.make_async_copy(piece, piece, rx_sem.at[1, q]).wait()
-        cp = pltpu.make_async_remote_copy(piece, piece, sg_sem.at[q], rg_sem.at[q],
-                                          device_id=dev_id(x * 2 + 1 - c, d), device_id_type=MESH)
-        cp.start()
-        forward.append(cp)
-    for q in range(nq):
-        piece = gf.at[pl.ds(pl.multiple_of(other + q * rows, 8), rows), :]
-        pltpu.make_async_copy(piece, piece, rg_sem.at[q]).wait()
+    for p, (r0, n) in enumerate(parts):
+        def wait_xy(k, carry, p=p, r0=r0, n=n):
+            q = (q_own + k) % nq
+            piece = rx.at[q, pl.ds(r0, n)]
+            pltpu.make_async_copy(piece, piece, rx_sem.at[0, p, q]).wait()
+            return carry
+
+        lax.fori_loop(1, nq, wait_xy, 0)
+        acc = rx[0, r0:r0 + n]
+        for q in range(1, nq):
+            acc += rx[q, r0:r0 + n]
+        zb[r0:r0 + n] = acc
+        for kz in range(1, nz):
+            send(zb.at[pl.ds(r0, n)], rz.at[z, pl.ds(r0, n)], sz_sem.at[p, kz], rz_sem.at[p, z],
+                 dev_id(g, y * nz + (z + kz) % nz))
+        rz[z, r0:r0 + n] = acc
+    for p, (r0, n) in enumerate(parts):
+        for kz in range(1, nz):
+            piece = rz.at[(z + kz) % nz, pl.ds(r0, n)]
+            pltpu.make_async_copy(piece, piece, rz_sem.at[p, (z + kz) % nz]).wait()
+        acc = rz[0, r0:r0 + n]
+        for k in range(1, nz):
+            acc += rz[k, r0:r0 + n]
+        gf[pl.ds(pl.multiple_of(own + q_own * rows + r0, 8), n), :] = acc
+        here = held(own + q_own * rows, r0, n)
+        for kx, ky in plane[1:]:
+            send(here, here, sx_sem.at[1, p, kx * ny + ky], rx_sem.at[1, p, q_own], at_peer(kx, ky)[1])
+    for p, (r0, n) in enumerate(parts):
+        for kx, ky in plane:
+            q = at_peer(kx, ky)[0]
+            piece = held(own + q * rows, r0, n)
+            if (kx, ky) != (0, 0):
+                pltpu.make_async_copy(piece, piece, rx_sem.at[1, p, q]).wait()
+            send(piece, piece, sg_sem.at[p, q], rg_sem.at[p, q], partner)
+    for p, (r0, n) in enumerate(parts):
+        for q in range(nq):
+            piece = held(other + q * rows, r0, n)
+            pltpu.make_async_copy(piece, piece, rg_sem.at[p, q]).wait()
     hb_rows = BLK // 2
     for idx in range(10):
         for h in range(2):
@@ -320,7 +330,7 @@
     out_ref[...] = own_part(work, d, g)
     for idx in range(10):
         to_core(idx).wait_send()
-    for cp in sends + xy_cps + z_cps + ag_cps + forward:
+    for cp in sends + later:
         cp.wait_send()
 
 
@@ -330,6 +340,7 @@
     nq = nx * ny
     half = 5 * BLK
     rows = half // nq
+    np_ = len(PARTS)
     cfg = (nx, ny, nz, jl, scale)
     f32, bf16 = jnp.float32, jnp.bfloat16
     dma = pltpu.SemaphoreType.DMA
@@ -352,13 +363,13 @@
             pltpu.VMEM((nz, rows, BLK), f32),
             pltpu.VMEM((2 * half, BLK), f32),
             pltpu.VMEM((2 * half, BLK), f32),
-            pltpu.VMEM((BLK, BLK), f32),
+            pltpu.VMEM((2, BLK, BLK), f32),
             dma((ny,)),
             dma((ny, nz)), dma((ny * nz,)),
             dma((10,)), dma((10,)),
-            dma((2, nq)), dma((2, nq)),
-            dma((nz,)), dma((nz,)),
-            dma((nq,)), dma((nq,)),
+            dma((2, np_, nq)), dma((2, np_, nq)),
+            dma((np_, nz)), dma((np_, nz)),
+            dma((np_, nq)), dma((np_, nq)),
             dma(()),
             pltpu.SemaphoreType.REGULAR((ny,)),
         ],

time: 75.3 us -> 73.4 us (0.975)
  Pallas kernels: 73.7 us -> 71.9 us
    pallas_call x1, Pallas kernels: 73.7 us -> 71.9 us  [triangle(): pl.pallas_call(functools.partial(gram_body, cfg), out_shape=jax.ShapeDtyp...]
where the time goes in v5:
time: 73.4 us; the launch traced here: 73.3 us
  Pallas kernels  71.9 us (98%)
  local copies, waits for them, and re-layouts  1.44 us (2%)
    pallas_call x1, Pallas kernels, triangle(): pl.pallas_call(functools.partial(gram_body, cfg), out_shape=jax.ShapeDtyp...  71.9 us

profile of v5, /device:TPU:1, one launch (start us, length us, event | category | flops | bytes accessed | tf_op | source)
XLA Modules:
  0.0 73.3 jit_solution(1120627671796480122)
XLA Ops:
  0.0 0.0 copy-start
  0.0 0.8 %copy-done = bf16[512,64]{0,1:T(8,128)(2,1)S(1)} copy-done((bf16[512,64]{0,1:T(8,128)(2,1)S(1)}, bf16[512,64]{0,1:T(8,128)(2,1)}, u32[]{:S(2)}) %copy-start) | copy-done | bytes 65560
  0.8 71.9 %shard_map.28 = f32[16,64]{1,0:T(8,128)S(1)} custom-call(bf16[16,512,512]{2,1,0:T(8,128)(2,1)} %bitcast.5, bf16[64,512]{1,0:T(8,128)(2,1)S(1)} %bitcast.4), custom_call_target="tpu_custom_call" | custom-call | tf_op jit(solution)/shard_map/pallas_call | solution.py:347
  72.7 0.6 copy.4
Async XLA Ops:
  0.0 0.8 %copy-start = (bf16[512,64]{0,1:T(8,128)(2,1)S(1)}, bf16[512,64]{0,1:T(8,128)(2,1)}, u32[]{:S(2)}) copy-start(bf16[512,64]{0,1:T(8,128)(2,1)} %param.3) | copy-start | bytes 196612

commit v6 on v5

--- a/solution.py
+++ b/solution.py
@@ -89,8 +89,9 @@
     return lax.dot_general(lhs, rhs, (((1,), (0,)), ((), ())), preferred_element_type=jnp.float32)
 
 
-def cholesky_packed(g, inv):
+def cholesky_packed(g, inv, row, col):
     n = 4
+    mine, own_strip = row // 8, row % 8 // (STRIP // 16)
     eye = (lax.broadcasted_iota(jnp.int32, (BLK, BLK), 0) == lax.broadcasted_iota(jnp.int32, (BLK, BLK), 1)).astype(jnp.float32)
     def panel(k, b):
         o = block_at(k, b) * BLK
@@ -100,32 +101,40 @@
         o, oa, ob = (block_at(*ab) * BLK for ab in ((a, b), (k, a), (k, b)))
         g[o:o + BLK, :] = g[o:o + BLK, :] - gram_like(g[oa:oa + BLK, :], g[ob:ob + BLK, :])
 
-    for k in range(n):
-        base = block_at(k, k) * BLK
-        last = k == n - 1
-        way = inv.at[k % 2]
-        if not last:
-            way[...] = eye
-        refs = [(g, base)] if last else [(g, base), (way, 0)]
+    def strip(k, refs, s):
+        at = s * STRIP
+        tiles = [[r[o + at + i:o + at + i + 8, :] for i in range(0, STRIP, 8)] for r, o in refs]
+        done = factor_rows(tiles, at)
+        for (r, o), v in zip(refs, done):
+            r[o + at:o + at + STRIP, :] = v
+        end = at + STRIP
+        if end < BLK:
+            both = jnp.concatenate(done, axis=1) if len(done) > 1 else done[0]
+            upd = gram_like(done[0], both)
+            for i, (r, o) in enumerate(refs):
+                r[o + end:o + BLK, :] = r[o + end:o + BLK, :] - upd[end:, i * BLK:(i + 1) * BLK]
+
+    def block_row(k):
+        refs = [(g, block_at(k, k) * BLK)]
+        if k < n - 1:
+            inv[k % 2] = eye
+            refs.append((inv.at[k % 2], 0))
         for s in range(BLK // STRIP):
-            at = s * STRIP
-            tiles = [[r[o + at + i:o + at + i + 8, :] for i in range(0, STRIP, 8)] for r, o in refs]
-            done = factor_rows(tiles, at)
-            for (r, o), v in zip(refs, done):
-                r[o + at:o + at + STRIP, :] = v
-            end = at + STRIP
-            if end < BLK:
-                both = done[0] if last else jnp.concatenate(done, axis=1)
-                upd = gram_like(done[0], both)
-                for i, (r, o) in enumerate(refs):
-                    r[o + end:o + BLK, :] = r[o + end:o + BLK, :] - upd[end:, i * BLK:(i + 1) * BLK]
-        if last:
-            break
+            pl.when((mine - k) * (BLK // STRIP) + own_strip >= s)(functools.partial(strip, k, refs, s))
         for b in range(k + 1, n):
             panel(k, b)
-        for a in range(k + 1, n):
-            for b in range(a, n):
-                update(k, a, b)
+
+        if k < n - 1:
+            @pl.when(mine > k)
+            def _():
+                for a in range(k + 1, n):
+                    for b in range(a, n):
+                        update(k, a, b)
+
+    @pl.when(col // 2 >= mine)
+    def _():
+        for k in range(n):
+            pl.when(mine >= k)(functools.partial(block_row, k))
 
 
 def own_part(g, row, col):
@@ -326,7 +335,7 @@
     for idx in range(10):
         for h in range(2):
             work[idx * BLK + h * hb_rows:idx * BLK + (h + 1) * hb_rows, :] = gf[h * half + idx * hb_rows:h * half + (idx + 1) * hb_rows, :]
-    cholesky_packed(work, inv)
+    cholesky_packed(work, inv, d, g)
     out_ref[...] = own_part(work, d, g)
     for idx in range(10):
         to_core(idx).wait_send()

time: 73.4 us -> 70 us (0.954)
  the two profiles are of different devices: /device:TPU:1 before, /device:TPU:31 now
where the time goes in v6:
time: 70 us; the launch traced here: 69.9 us
  Pallas kernels  68.4 us (98%)
  local copies, waits for them, and re-layouts  1.44 us (2%)
    pallas_call x1, Pallas kernels, triangle(): pl.pallas_call(functools.partial(gram_body, cfg), out_shape=jax.ShapeDtyp...  68.4 us
    unnamed x3, local copies, waits for them, and re-layouts  1.44 us

profile of v6, /device:TPU:31, one launch (start us, length us, event | category | flops | bytes accessed | tf_op | source)
XLA Modules:
  0.0 69.9 jit_solution(8484575399129597498)
XLA Ops:
  0.0 0.0 copy-start
  0.0 0.8 %copy-done = bf16[512,64]{0,1:T(8,128)(2,1)S(1)} copy-done((bf16[512,64]{0,1:T(8,128)(2,1)S(1)}, bf16[512,64]{0,1:T(8,128)(2,1)}, u32[]{:S(2)}) %copy-start) | copy-done | bytes 65560
  0.8 68.4 %shard_map.28 = f32[16,64]{1,0:T(8,128)S(1)} custom-call(bf16[16,512,512]{2,1,0:T(8,128)(2,1)} %bitcast.5, bf16[64,512]{1,0:T(8,128)(2,1)S(1)} %bitcast.4), custom_call_target="tpu_custom_call" | custom-call | tf_op jit(solution)/shard_map/pallas_call | solution.py:356
  69.3 0.6 copy.4
Async XLA Ops:
  0.0 0.8 %copy-start = (bf16[512,64]{0,1:T(8,128)(2,1)S(1)}, bf16[512,64]{0,1:T(8,128)(2,1)}, u32[]{:S(2)}) copy-start(bf16[512,64]{0,1:T(8,128)(2,1)} %param.3) | copy-start | bytes 196612

commit v7 on v6

--- a/solution.py
+++ b/solution.py
@@ -101,12 +101,14 @@
         o, oa, ob = (block_at(*ab) * BLK for ab in ((a, b), (k, a), (k, b)))
         g[o:o + BLK, :] = g[o:o + BLK, :] - gram_like(g[oa:oa + BLK, :], g[ob:ob + BLK, :])
 
-    def strip(k, refs, s):
+    def strip(k, refs, s, height=STRIP):
         at = s * STRIP
-        tiles = [[r[o + at + i:o + at + i + 8, :] for i in range(0, STRIP, 8)] for r, o in refs]
+        tiles = [[r[o + at + i:o + at + i + 8, :] for i in range(0, height, 8)] for r, o in refs]
         done = factor_rows(tiles, at)
         for (r, o), v in zip(refs, done):
-            r[o + at:o + at + STRIP, :] = v
+            r[o + at:o + at + height, :] = v
+        if height < STRIP:
+            return
         end = at + STRIP
         if end < BLK:
             both = jnp.concatenate(done, axis=1) if len(done) > 1 else done[0]
@@ -120,7 +122,11 @@
             inv[k % 2] = eye
             refs.append((inv.at[k % 2], 0))
         for s in range(BLK // STRIP):
-            pl.when((mine - k) * (BLK // STRIP) + own_strip >= s)(functools.partial(strip, k, refs, s))
+            if k < n - 1:
+                pl.when((mine - k) * (BLK // STRIP) + own_strip >= s)(functools.partial(strip, k, refs, s))
+            else:
+                pl.when(row % 8 > 2 * s)(functools.partial(strip, k, refs, s))
+                pl.when(row % 8 == 2 * s)(functools.partial(strip, k, refs, s, STRIP // 2))
         for b in range(k + 1, n):
             panel(k, b)
 

time: 70 us -> 69.5 us (level)
  no operation moved by 1% of the time
where the time goes in v7:
time: 69.5 us; the launch traced here: 69.4 us
  Pallas kernels  68 us (98%)
  local copies, waits for them, and re-layouts  1.44 us (2%)
    pallas_call x1, Pallas kernels, triangle(): pl.pallas_call(functools.partial(gram_body, cfg), out_shape=jax.ShapeDtyp...  68 us
    unnamed x3, local copies, waits for them, and re-layouts  1.44 us

profile of v7, /device:TPU:31, one launch (start us, length us, event | category | flops | bytes accessed | tf_op | source)
XLA Modules:
  0.0 69.4 jit_solution(16214821646973822303)
XLA Ops:
  0.0 0.0 copy-start
  0.0 0.8 %copy-done = bf16[512,64]{0,1:T(8,128)(2,1)S(1)} copy-done((bf16[512,64]{0,1:T(8,128)(2,1)S(1)}, bf16[512,64]{0,1:T(8,128)(2,1)}, u32[]{:S(2)}) %copy-start) | copy-done | bytes 65560
  0.8 68.0 %shard_map.28 = f32[16,64]{1,0:T(8,128)S(1)} custom-call(bf16[16,512,512]{2,1,0:T(8,128)(2,1)} %bitcast.5, bf16[64,512]{1,0:T(8,128)(2,1)S(1)} %bitcast.4), custom_call_target="tpu_custom_call" | custom-call | tf_op jit(solution)/shard_map/pallas_call | solution.py:362
  68.8 0.6 copy.4
Async XLA Ops:
  0.0 0.8 %copy-start = (bf16[512,64]{0,1:T(8,128)(2,1)S(1)}, bf16[512,64]{0,1:T(8,128)(2,1)}, u32[]{:S(2)}) copy-start(bf16[512,64]{0,1:T(8,128)(2,1)} %param.3) | copy-start | bytes 196612
